TPU v7x, 32 devices: a whole 2x2x4 slice. The times are simulated.
32 devices in a mesh: mat: 8 (over z, core), pts: 4 (over y, x).
Axes of the slice: x: 2, y: 2, z: 4, core: 2. Of those that a mesh axis runs over, the one named last changes fastest.
Arguments:
- dens_blocks: bfloat16 [8, 2048, 2048], P(None, 'pts', 'mat'), may hold values from -0.00390625 to 0.00390625
- basis_values: bfloat16 [8, 6144, 1536], P('mat', 'pts'), may hold values from -6 to 6
- kernel: float32 [8, 6144], P('mat', 'pts'), may hold values from 0.3 to 3
- perturbation: float32 [8, 6144], P('mat', 'pts'), may hold values from -6 to 6
- quad_weight: float32 [8, 6144], P('mat', 'pts'), may hold values from 0.002 to 0.02
- point_count: int32 [8, 4], P('mat', 'pts'), may hold values from 192 to 1536, as said below
- active_blocks: int32 [8, 4, 12], P('mat', 'pts'), may hold values from 0 to 15, as said below
- block_pattern: int32 [8, 16, 16], replicated, may hold values 0 or 1
Outputs:
- h_response: float32 [8, 2048, 2048], P(None, 'pts', 'mat')
- n_response: float32 [8, 6144], P('mat', 'pts')
Inputs may be any that keep to these rules, and one draw needn't show every extreme that they name: `point_count`: each cluster has at least one shard with exactly 1536 points in use; the others hold 192 or more. `active_blocks`: the 12 entries of one shard are distinct block numbers of its cluster, in no particular order.
All inputs are finite; a program needn't handle non-finite values.
Results may differ from a plain program's by a relative error of at most 0.011.
Values may be sent and summed in bfloat16 or wider, within the bound.
No kernel may reach another device: no remote copies, remote signals or barrier semaphores. Data moves between devices by JAX's collectives and lax.ppermute only.
A program may use at most 128 MiB of HBM per device.

v0:
```python
import functools

import jax
import jax.numpy as jnp
from jax import lax
from jax.experimental import pallas as pl
from jax.experimental.pallas import tpu as pltpu
from jax.sharding import PartitionSpec as P


BLOCK = 128
VM = pl.BlockSpec(memory_space=pltpu.VMEM)
ANY = pl.BlockSpec(memory_space=pl.ANY)
HEAD = 3
GRANT = pltpu.CompilerParams(vmem_limit_bytes=20 << 20)


def cost(flops, moved):
    return pl.CostEstimate(flops=int(flops), bytes_accessed=int(moved), transcendentals=0)


def lanes(block):
    return pl.ds(pl.multiple_of(block * BLOCK, BLOCK), BLOCK)


def pack_kernel(dims, start, meta, *refs):
    n_mat, n_pts, act, nact = dims
    arrived, packed, stage = refs[:n_mat], refs[n_mat:-1], refs[-1]
    width = arrived[0].shape[1]
    for d in range(n_mat):
        stage[:, pl.ds(pl.multiple_of((meta[0] ^ d) * width, BLOCK), width)] = arrived[d][...]
    row_block = meta[1] * (act // n_pts) + start // BLOCK
    pattern_at = HEAD + n_pts * nact + row_block * act
    for o in range(n_pts):
        for j in range(nact):
            b = meta[HEAD + o * nact + j]
            keep = meta[pattern_at + b] != 0
            value = stage[:, lanes(b)]
            packed[o][:, j * BLOCK : (j + 1) * BLOCK] = jnp.where(keep, value, jnp.zeros_like(value))


def pack(dims, start, rows, meta, arrived, skip):
    n_mat, n_pts, act, nact = dims
    width = act // n_mat * BLOCK
    return pl.pallas_call(
        functools.partial(pack_kernel, dims, start),
        out_shape=[jax.ShapeDtypeStruct((rows, nact * BLOCK), jnp.bfloat16)] * n_pts,
        grid_spec=pltpu.PrefetchScalarGridSpec(
            num_scalar_prefetch=1,
            grid=(1,),
            in_specs=[pl.BlockSpec((rows, width), lambda i, meta: (skip // rows, 0))] * n_mat,
            out_specs=[pl.BlockSpec((rows, nact * BLOCK), lambda i, meta: (0, 0))] * n_pts,
            scratch_shapes=[pltpu.VMEM((rows, act * BLOCK), jnp.bfloat16)],
        ),
        compiler_params=GRANT,
        cost_estimate=cost(0, 2 * rows * BLOCK * (act + n_pts * nact)),
    )(meta, *arrived)


def transpose_kernel(given, out):
    out[...] = given[...].T


def transposed(basis):
    points, orbitals = basis.shape
    tile = 256
    return pl.pallas_call(
        transpose_kernel,
        out_shape=jax.ShapeDtypeStruct((orbitals, points), basis.dtype),
        grid=(points // tile,),
        in_specs=[pl.BlockSpec((tile, orbitals), lambda i: (i, 0))],
        out_specs=pl.BlockSpec((orbitals, tile), lambda i: (0, i)),
        compiler_params=GRANT,
        cost_estimate=cost(0, 4 * points * orbitals),
        name="flip",
    )(basis)


def invert(dims, meta, place):
    _, _, act, nact = dims
    for a in range(act):
        place[a] = -1
    for i in range(nact):
        place[meta[HEAD + i]] = i


def rows_of(place, block, start, rows):
    spot = place[block]
    at = jnp.maximum(spot, 0) * BLOCK + start % BLOCK
    return pl.ds(pl.multiple_of(at, rows), rows), spot >= 0


def density_kernel(dims, start, rows, tile, last, meta, *refs):
    _, n_pts, act, _ = dims
    parts, flipped, before, after, place = refs[:n_pts], refs[n_pts], refs[n_pts + 1], refs[n_pts + 2], refs[n_pts + 3]
    invert(dims, meta, place)
    left = jnp.concatenate([part[...] for part in parts], axis=0)
    points = flipped.shape[1]

    @pl.loop(0, points // tile)
    def _(t):
        at = pl.ds(pl.multiple_of(t * tile, tile), tile)
        inner = jnp.dot(left, flipped[:, at], preferred_element_type=jnp.float32)
        total = before[:, at]
        for o in range(n_pts):
            where, active = rows_of(place, (meta[1] ^ o) * (act // n_pts) + start // BLOCK, start, rows)
            own = flipped[where, at].astype(jnp.float32)
            share = jnp.sum(inner[o * rows : (o + 1) * rows] * own, axis=0, keepdims=True)
            total = total + jnp.where(active, share, jnp.zeros_like(share))
        if last:
            point = t * tile + lax.broadcasted_iota(jnp.int32, total.shape, 1)
            total = jnp.where(point < meta[2], total, jnp.zeros_like(total))
        after[:, at] = total


def density(dims, start, rows, last, meta, parts, flipped, before):
    _, n_pts, act, _ = dims
    orbitals, points = flipped.shape
    return pl.pallas_call(
        functools.partial(density_kernel, dims, start, rows, 256, last),
        out_shape=jax.ShapeDtypeStruct((1, points), jnp.float32),
        in_specs=[pl.BlockSpec(memory_space=pltpu.SMEM)] + [VM] * (n_pts + 2),
        out_specs=VM,
        scratch_shapes=[pltpu.SMEM((act,), jnp.int32)],
        compiler_params=GRANT,
        cost_estimate=cost(2 * n_pts * rows * orbitals * points, 2 * orbitals * points),
    )(meta, *parts, flipped, before)


def response_kernel(dims, start, rows, tile, meta, *refs):
    _, n_pts, act, _ = dims
    flipped, basis, n, kern, pert, weight = refs[:6]
    out, place, left = refs[6 : 6 + n_pts], refs[-2], refs[-1]
    invert(dims, meta, place)
    points = flipped.shape[1]
    inside = lax.broadcasted_iota(jnp.int32, (1, points), 1) < meta[2]
    scaling = jnp.where(inside, weight[...] * (pert[...] - kern[...] * n[...]), 0.0)
    for o in range(n_pts):
        where, active = rows_of(place, (meta[1] ^ o) * (act // n_pts) + start // BLOCK, start, rows)
        own = flipped[where, :].astype(jnp.float32)
        left[o * rows : (o + 1) * rows, :] = jnp.where(active, own * scaling, 0.0).astype(jnp.bfloat16)

    @pl.loop(0, basis.shape[1] // tile)
    def _(t):
        at = pl.ds(pl.multiple_of(t * tile, tile), tile)
        block = jnp.dot(left[...], basis[:, at], preferred_element_type=jnp.float32)
        for o in range(n_pts):
            out[o][:, at] = block[o * rows : (o + 1) * rows].astype(jnp.bfloat16)


def response(dims, start, rows, meta, flipped, basis, n, kern, pert, weight):
    _, n_pts, act, _ = dims
    orbitals, points = flipped.shape
    return pl.pallas_call(
        functools.partial(response_kernel, dims, start, rows, 256),
        out_shape=[jax.ShapeDtypeStruct((rows, orbitals), jnp.bfloat16)] * n_pts,
        in_specs=[pl.BlockSpec(memory_space=pltpu.SMEM)] + [VM] * 6,
        out_specs=[VM] * n_pts,
        scratch_shapes=[
            pltpu.SMEM((act,), jnp.int32),
            pltpu.VMEM((n_pts * rows, points), jnp.bfloat16),
        ],
        compiler_params=GRANT,
        cost_estimate=cost(2 * n_pts * rows * orbitals * points, 4 * orbitals * points),
    )(meta, flipped, basis, n, kern, pert, weight)


def combine_kernel(dims, strips, meta, *refs):
    n_mat, n_pts, act, nact = dims
    given = len(strips) * n_pts
    out, total = refs[given:-1], refs[-1]
    each = act // n_mat
    done = 0
    for s, (start, rows) in enumerate(strips):
        total[...] = jnp.zeros_like(total)
        for o in range(n_pts):
            part = refs[s * n_pts + o]
            for j in range(nact):
                b = meta[HEAD + o * nact + j]
                total[:rows, lanes(b)] += part[:, j * BLOCK : (j + 1) * BLOCK].astype(jnp.float32)
        row_block = meta[1] * (act // n_pts) + start // BLOCK
        pattern_at = HEAD + n_pts * nact + row_block * act
        for d in range(n_mat):
            for k in range(each):
                b = (meta[0] ^ d) * each + k
                keep = meta[pattern_at + b] != 0
                value = total[:rows, lanes(b)]
                value = jnp.where(keep, value, jnp.zeros_like(value)).astype(jnp.bfloat16)
                out[d][done : done + rows, k * BLOCK : (k + 1) * BLOCK] = value
        done += rows


def combine(dims, strips, meta, given):
    n_mat, n_pts, act, nact = dims
    rows = sum(rows for start, rows in strips)
    return pl.pallas_call(
        functools.partial(combine_kernel, dims, strips),
        out_shape=[jax.ShapeDtypeStruct((rows, act // n_mat * BLOCK), jnp.bfloat16)] * n_mat,
        in_specs=[pl.BlockSpec(memory_space=pltpu.SMEM)] + [VM] * len(given),
        out_specs=[VM] * n_mat,
        scratch_shapes=[pltpu.VMEM((BLOCK, act * BLOCK), jnp.float32)],
        compiler_params=GRANT,
        cost_estimate=cost(0, 2 * rows * BLOCK * (act + n_pts * nact)),
    )(meta, *given)


def widen_kernel(n_mat, meta, *refs):
    out = refs[-1]
    for d in range(n_mat):
        out[meta[0] ^ d] = refs[d][...].astype(jnp.float32)


def widen(dims, start, rows, all_rows, meta, given, held):
    n_mat, _, act, _ = dims
    width = act // n_mat * BLOCK
    more = [] if held is None else [held]
    return pl.pallas_call(
        functools.partial(widen_kernel, n_mat),
        out_shape=jax.ShapeDtypeStruct((n_mat, all_rows, width), jnp.float32),
        grid_spec=pltpu.PrefetchScalarGridSpec(
            num_scalar_prefetch=1,
            grid=(1,),
            in_specs=[pl.BlockSpec((rows, width), lambda i, meta: (0, 0))] * n_mat + [ANY] * len(more),
            out_specs=pl.BlockSpec((n_mat, rows, width), lambda i, meta: (0, start // rows, 0)),
        ),
        input_output_aliases={} if held is None else {1 + n_mat: 0},
        compiler_params=GRANT,
        cost_estimate=cost(0, 6 * rows * n_mat * width),
    )(meta, *given, *more)


def chunks(row_blocks, shape):
    half = BLOCK // 2
    if sum(sum(sizes) for sizes in shape) != 2 * row_blocks:
        shape = [[2]] * row_blocks
    out, at = [], 0
    for sizes in shape:
        strips = []
        for size in sizes:
            strips.append((at, size * half))
            at += size * half
        out.append(tuple(strips))
    return out


def plan_of(row_blocks):
    inward = chunks(row_blocks, [[2], [2], [2, 1, 1]])
    outward = chunks(row_blocks, [[1, 1], [2], [2], [1, 1]])
    return inward, outward


def body(dens_blocks, basis_values, kernel, perturbation, quad_weight, point_count, active_blocks, block_pattern):
    n_mat, n_pts = lax.axis_size("mat"), lax.axis_size("pts")
    act, nact = block_pattern.shape[1], active_blocks.shape[2]
    dims = (n_mat, n_pts, act, nact)
    inward, outward = plan_of(act // n_pts)
    me_mat, me_pts = lax.axis_index("mat"), lax.axis_index("pts")

    def to_peer(value, o):
        return lax.ppermute(value, "pts", [(i, i ^ o) for i in range(n_pts)])

    points = basis_values.shape[1]
    basis = basis_values[0]
    own_active = active_blocks[0, 0]

    def across(values):
        out = [values[0]]
        for d in range(1, n_mat):
            out.append(lax.ppermute(values[d], "mat", [(i, i ^ d) for i in range(n_mat)]))
        return out

    arrived = {}
    for strips in inward:
        start, rows = strips[0][0], sum(rows for at, rows in strips)
        cut = [
            lax.dynamic_slice(dens_blocks, (me_mat ^ d, start, 0), (1, rows, dens_blocks.shape[2]))[0]
            for d in range(n_mat)
        ]
        arrived[start] = across(cut)

    peers = [own_active] + [to_peer(own_active, o) for o in range(1, n_pts)]
    pattern = lax.dynamic_index_in_dim(block_pattern, me_mat, 0, keepdims=False).reshape(-1)
    head = jnp.stack([me_mat, me_pts, point_count[0, 0]]).astype(jnp.int32)
    meta = jnp.concatenate([head] + peers + [pattern])

    flipped = transposed(basis)

    parts = {}
    for strips in inward:
        first = strips[0][0]
        for start, rows in strips:
            packed = pack(dims, start, rows, meta, arrived[first], start - first)
            parts[start] = [packed[0]] + [to_peer(packed[o], o) for o in range(1, n_pts)]

    n = jnp.zeros((1, points), jnp.float32)
    for strips in inward:
        for start, rows in strips:
            last = start + rows == dens_blocks.shape[1]
            n = density(dims, start, rows, last, meta, parts[start], flipped, n)

    given = {}
    for strips in outward:
        for start, rows in strips:
            sent = response(dims, start, rows, meta, flipped, basis, n, kernel, perturbation, quad_weight)
            given[start] = [sent[0]] + [to_peer(sent[o], o) for o in range(1, n_pts)]

    held = None
    for strips in outward:
        start, rows = strips[0][0], sum(rows for at, rows in strips)
        cut = combine(dims, strips, meta, sum([given[at] for at, rows in strips], []))
        back = across(cut)
        held = widen(dims, start, rows, dens_blocks.shape[1], meta, back, held)
    return held, n


def solution(mesh):
    placed = (
        P(None, "pts", "mat"),
        P("mat", "pts", None),
        P("mat", "pts"),
        P("mat", "pts"),
        P("mat", "pts"),
        P("mat", "pts"),
        P("mat", "pts", None),
        P(),
    )

    return jax.shard_map(
        body,
        mesh=mesh,
        in_specs=placed,
        out_specs=(P(None, "pts", "mat"), P("mat", "pts")),
        check_vma=False,
    )
```

profile of v0, /device:TPU:0, one launch (start us, length us, event | category | flops | bytes accessed | tf_op | source)
XLA Modules:
  0.0 245.6 jit_solution(14326146857709416845)
XLA Ops:
  0.7 4.0 %collective-permute-start.2 = (s32[12]{0:T(128)}, s32[12]{0:T(128)S(1)}, u32[]{:S(2)}, u32[]{:S(2)}) collective-permute-start(s32[12]{0:T(128)} %bitcast.63), channel_id=1, source_target_pairs={{0,3},{1,2},{2,1},{3,0},{4,7},{5,6},{6,5},{7,4},{8,11},{9,10},{10,... | collective-permute-start | bytes 152 | tf_op jit(solution)/shard_map/ppermute | solution.py:260
  6.5 2.5 %collective-permute-start.35 = (bf16[128,256]{1,0:T(8,128)(2,1)S(1)}, bf16[128,256]{1,0:T(8,128)(2,1)S(1)}, u32[]{:S(2)}, u32[]{:S(2)}) collective-permute-start(bf16[128,256]{1,0:T(8,128)(2,1)S(1)} %get-tuple-element.154), channel_id=1, source_target_pairs={{0,28},{4,24},{8,20},{12,16},{16,12},{20,8},{24,4},{28,0},{1,29},{... | collective-permute-start | bytes 196616 | tf_op jit(solution)/shard_map/ppermute | solution.py:269
  9.5 3.5 %collective-permute-start.32 = (bf16[128,256]{1,0:T(8,128)(2,1)S(1)}, bf16[128,256]{1,0:T(8,128)(2,1)S(1)}, u32[]{:S(2)}, u32[]{:S(2)}) collective-permute-start(bf16[128,256]{1,0:T(8,128)(2,1)S(1)} %get-tuple-element.156), channel_id=1, source_target_pairs={{0,16},{4,20},{8,24},{12,28},{16,0},{20,4},{24,8},{28,12},{1,17},{... | collective-permute-start | bytes 196616 | tf_op jit(solution)/shard_map/ppermute | solution.py:269
  14.9 2.6 %collective-permute-done.33.refs_5_ = bf16[128,256]{1,0:T(8,128)(2,1)S(1)} collective-permute-done((bf16[128,256]{1,0:T(8,128)(2,1)S(1)}, bf16[128,256]{1,0:T(8,128)(2,1)S(1)}, u32[]{:S(2)}, u32[]{:S(2)}) %collective-permute-start.33) | collective-permute-done | bytes 65568 | tf_op jit(solution)/shard_map/ppermute | solution.py:269
  29.5 3.2 %collective-permute-done.23.refs_5_ = bf16[128,256]{1,0:T(8,128)(2,1)S(1)} collective-permute-done((bf16[128,256]{1,0:T(8,128)(2,1)S(1)}, bf16[128,256]{1,0:T(8,128)(2,1)S(1)}, u32[]{:S(2)}, u32[]{:S(2)}) %collective-permute-start.23) | collective-permute-done | bytes 65568 | tf_op jit(solution)/shard_map/ppermute | solution.py:269
  36.9 3.6 %collective-permute-done.34.refs_6_ = bf16[128,256]{1,0:T(8,128)(2,1)S(1)} collective-permute-done((bf16[128,256]{1,0:T(8,128)(2,1)S(1)}, bf16[128,256]{1,0:T(8,128)(2,1)S(1)}, u32[]{:S(2)}, u32[]{:S(2)}) %collective-permute-start.34) | collective-permute-done | bytes 65568 | tf_op jit(solution)/shard_map/ppermute | solution.py:269
  48.3 5.1 %collective-permute-start.4 = (bf16[256,256]{1,0:T(8,128)(2,1)S(1)}, bf16[256,256]{1,0:T(8,128)(2,1)S(1)}, u32[]{:S(2)}, u32[]{:S(2)}) collective-permute-start(bf16[256,256]{1,0:T(8,128)(2,1)S(1)} %get-tuple-element.175), channel_id=1, source_target_pairs={{0,8},{4,12},{8,0},{12,4},{16,24},{20,28},{24,16},{28,20},{1,9},{5... | collective-permute-start | bytes 393224 | tf_op jit(solution)/shard_map/ppermute | solution.py:269
  71.1 4.5 %collective-permute-done.37.refs_2_ = bf16[128,1536]{1,0:T(8,128)(2,1)S(1)} collective-permute-done((bf16[128,1536]{1,0:T(8,128)(2,1)S(1)}, bf16[128,1536]{1,0:T(8,128)(2,1)S(1)}, u32[]{:S(2)}, u32[]{:S(2)}) %collective-permute-start.37) | collective-permute-done | bytes 393248 | tf_op jit(solution)/shard_map/ppermute | solution.py:260
  79.7 4.2 %shard_map.100.refs_5_ = f32[1,1536]{1,0:T(1,128)S(1)} custom-call(s32[307]{0:T(512)S(1)} %concatenate.3.meta, bf16[128,1536]{1,0:T(8,128)(2,1)S(1)} %get-tuple-element.94.refs_0_, bf16[128,1536]{1,0:T(8,128)(2,1)S(1)} %collective-permute-done.36.refs_1_, bf16[128,1536]{1,0:T(8,128)(2,1)S(1)} %collective-permute-done.37.refs_2_, ...), custom_call_target="tpu_custom_call" | custom-call | flops 2415919104 | bytes 4718592 | tf_op jit(solution)/shard_map/pallas_call | solution.py:119
  84.0 8.5 %collective-permute-done.27.refs_2_ = bf16[128,1536]{1,0:T(8,128)(2,1)S(1)} collective-permute-done((bf16[128,1536]{1,0:T(8,128)(2,1)S(1)}, bf16[128,1536]{1,0:T(8,128)(2,1)S(1)}, u32[]{:S(2)}, u32[]{:S(2)}) %collective-permute-start.27) | collective-permute-done | bytes 393248 | tf_op jit(solution)/shard_map/ppermute | solution.py:260
  95.1 4.2 %shard_map.101.refs_5_ = f32[1,1536]{1,0:T(1,128)S(1)} custom-call(s32[307]{0:T(512)S(1)} %concatenate.3.meta, bf16[128,1536]{1,0:T(8,128)(2,1)S(1)} %get-tuple-element.90.refs_0_, bf16[128,1536]{1,0:T(8,128)(2,1)S(1)} %collective-permute-done.26.refs_1_, bf16[128,1536]{1,0:T(8,128)(2,1)S(1)} %collective-permute-done.27.refs_2_, ...), custom_call_target="tpu_custom_call" | custom-call | flops 2415919104 | bytes 4718592 | tf_op jit(solution)/shard_map/pallas_call | solution.py:119
  99.3 8.9 %collective-permute-done.13.refs_1_ = bf16[64,1536]{1,0:T(8,128)(2,1)S(1)} collective-permute-done((bf16[64,1536]{1,0:T(8,128)(2,1)S(1)}, bf16[64,1536]{1,0:T(8,128)(2,1)S(1)}, u32[]{:S(2)}, u32[]{:S(2)}) %collective-permute-start.13) | collective-permute-done | bytes 196640 | tf_op jit(solution)/shard_map/ppermute | solution.py:260
  114.0 4.2 %shard_map.102.refs_5_ = f32[1,1536]{1,0:T(1,128)S(1)} custom-call(s32[307]{0:T(512)S(1)} %concatenate.3.meta, bf16[128,1536]{1,0:T(8,128)(2,1)S(1)} %get-tuple-element.86.refs_0_, bf16[128,1536]{1,0:T(8,128)(2,1)S(1)} %collective-permute-done.16.refs_1_, bf16[128,1536]{1,0:T(8,128)(2,1)S(1)} %collective-permute-done.17.refs_2_, ...), custom_call_target="tpu_custom_call" | custom-call | flops 2415919104 | bytes 4718592 | tf_op jit(solution)/shard_map/pallas_call | solution.py:119
  118.3 3.0 %shard_map.103.refs_5_ = f32[1,1536]{1,0:T(1,128)S(1)} custom-call(s32[307]{0:T(512)S(1)} %concatenate.3.meta, bf16[64,1536]{1,0:T(8,128)(2,1)S(1)} %get-tuple-element.82.refs_0_, bf16[64,1536]{1,0:T(8,128)(2,1)S(1)} %collective-permute-done.13.refs_1_, bf16[64,1536]{1,0:T(8,128)(2,1)S(1)} %collective-permute-done.14.refs_2_, ...), custom_call_target="tpu_custom_call" | custom-call | flops 1207959552 | bytes 4718592 | tf_op jit(solution)/shard_map/pallas_call | solution.py:119
  121.3 4.3 %collective-permute-done.11.refs_2_ = bf16[64,1536]{1,0:T(8,128)(2,1)S(1)} collective-permute-done((bf16[64,1536]{1,0:T(8,128)(2,1)S(1)}, bf16[64,1536]{1,0:T(8,128)(2,1)S(1)}, u32[]{:S(2)}, u32[]{:S(2)}) %collective-permute-start.11) | collective-permute-done | bytes 196640 | tf_op jit(solution)/shard_map/ppermute | solution.py:260
  125.5 3.6 %shard_map.104.refs_2_ = f32[1,1536]{1,0:T(1,128)} custom-call(s32[307]{0:T(512)S(1)} %concatenate.3.meta, bf16[64,1536]{1,0:T(8,128)(2,1)S(1)} %get-tuple-element.78.refs_0_, bf16[64,1536]{1,0:T(8,128)(2,1)S(1)} %collective-permute-done.10.refs_1_, bf16[64,1536]{1,0:T(8,128)(2,1)S(1)} %collective-permute-done.11.refs_2_, ...), custom_call_target="tpu_custom_call" | custom-call | flops 1207959552 | bytes 4718592 | tf_op jit(solution)/shard_map/pallas_call | solution.py:119
  129.8 3.0 %shard_map.113 = (bf16[64,1536]{1,0:T(8,128)(2,1)S(1)}, bf16[64,1536]{1,0:T(8,128)(2,1)S(1)}, bf16[64,1536]{1,0:T(8,128)(2,1)S(1)}, bf16[64,1536]{1,0:T(8,128)(2,1)S(1)}) custom-call(s32[307]{0:T(512)S(1)} %concatenate.3.meta, bf16[1536,1536]{1,0:T(8,128)(2,1)S(1)} %flip.1.refs_4_.refs_0_, bf16[1536,1536]{1,0:T(8,128)(2,1)S(1)} %bitcast.57, ...), custom_call_target="tpu_custom_call" | custom-call | flops 1207959552 | bytes 9437184 | tf_op jit(solution)/shard_map/pallas_call | solution.py:154
  136.4 3.0 %shard_map.112 = (bf16[64,1536]{1,0:T(8,128)(2,1)S(1)}, bf16[64,1536]{1,0:T(8,128)(2,1)S(1)}, bf16[64,1536]{1,0:T(8,128)(2,1)S(1)}, bf16[64,1536]{1,0:T(8,128)(2,1)S(1)}) custom-call(s32[307]{0:T(512)S(1)} %concatenate.3.meta, bf16[1536,1536]{1,0:T(8,128)(2,1)S(1)} %flip.1.refs_4_.refs_0_, bf16[1536,1536]{1,0:T(8,128)(2,1)S(1)} %bitcast.58, ...), custom_call_target="tpu_custom_call" | custom-call | flops 1207959552 | bytes 9437184 | tf_op jit(solution)/shard_map/pallas_call | solution.py:154
  139.6 3.0 %shard_map.106 = (bf16[64,1536]{1,0:T(8,128)(2,1)S(1)}, bf16[64,1536]{1,0:T(8,128)(2,1)S(1)}, bf16[64,1536]{1,0:T(8,128)(2,1)S(1)}, bf16[64,1536]{1,0:T(8,128)(2,1)S(1)}) custom-call(s32[307]{0:T(512)S(1)} %concatenate.3.meta, bf16[1536,1536]{1,0:T(8,128)(2,1)S(1)} %flip.1.refs_4_.refs_0_, bf16[1536,1536]{1,0:T(8,128)(2,1)S(1)} %bitcast.59, ...), custom_call_target="tpu_custom_call" | custom-call | flops 1207959552 | bytes 9437184 | tf_op jit(solution)/shard_map/pallas_call | solution.py:154
  146.2 3.0 %shard_map.105 = (bf16[64,1536]{1,0:T(8,128)(2,1)S(1)}, bf16[64,1536]{1,0:T(8,128)(2,1)S(1)}, bf16[64,1536]{1,0:T(8,128)(2,1)S(1)}, bf16[64,1536]{1,0:T(8,128)(2,1)S(1)}) custom-call(s32[307]{0:T(512)S(1)} %concatenate.3.meta, bf16[1536,1536]{1,0:T(8,128)(2,1)S(1)} %flip.1.refs_4_.refs_0_, bf16[1536,1536]{1,0:T(8,128)(2,1)S(1)} %bitcast.60, ...), custom_call_target="tpu_custom_call" | custom-call | flops 1207959552 | bytes 9437184 | tf_op jit(solution)/shard_map/pallas_call | solution.py:154
  159.1 4.4 %shard_map.110 = (bf16[128,1536]{1,0:T(8,128)(2,1)S(1)}, bf16[128,1536]{1,0:T(8,128)(2,1)S(1)}, bf16[128,1536]{1,0:T(8,128)(2,1)S(1)}, bf16[128,1536]{1,0:T(8,128)(2,1)S(1)}) custom-call(s32[307]{0:T(512)S(1)} %concatenate.3.meta, bf16[1536,1536]{1,0:T(8,128)(2,1)S(1)} %flip.1.refs_4_.refs_0_, bf16[1536,1536]{1,0:T(8,128)(2,1)S(1)} %bitcast.61, ...), custom_call_target="tpu_custom_call" | custom-call | flops 2415919104 | bytes 9437184 | tf_op jit(solution)/shard_map/pallas_call | solution.py:154
  173.9 2.6 %collective-permute-done.81.refs_4_ = bf16[128,256]{1,0:T(8,128)(2,1)S(1)} collective-permute-done((bf16[128,256]{1,0:T(8,128)(2,1)S(1)}, bf16[128,256]{1,0:T(8,128)(2,1)S(1)}, u32[]{:S(2)}, u32[]{:S(2)}) %collective-permute-start.81) | collective-permute-done | bytes 65568 | tf_op jit(solution)/shard_map/ppermute | solution.py:269
  178.1 4.6 %shard_map.108 = (bf16[128,1536]{1,0:T(8,128)(2,1)S(1)}, bf16[128,1536]{1,0:T(8,128)(2,1)S(1)}, bf16[128,1536]{1,0:T(8,128)(2,1)S(1)}, bf16[128,1536]{1,0:T(8,128)(2,1)S(1)}) custom-call(s32[307]{0:T(512)S(1)} %concatenate.3.meta, bf16[1536,1536]{1,0:T(8,128)(2,1)S(1)} %flip.1.refs_4_.refs_0_, bf16[1536,1536]{1,0:T(8,128)(2,1)S(1)} %bitcast.62, ...), custom_call_target="tpu_custom_call" | custom-call | flops 2415919104 | bytes 9437184 | tf_op jit(solution)/shard_map/pallas_call | solution.py:154
  187.9 3.8 %collective-permute-done.63.refs_2_ = bf16[128,1536]{1,0:T(8,128)(2,1)S(1)} collective-permute-done((bf16[128,1536]{1,0:T(8,128)(2,1)S(1)}, bf16[128,1536]{1,0:T(8,128)(2,1)S(1)}, u32[]{:S(2)}, u32[]{:S(2)}) %collective-permute-start.63) | collective-permute-done | bytes 393248 | tf_op jit(solution)/shard_map/ppermute | solution.py:260
  194.9 2.4 collective-permute-done.84.refs_7_
  199.4 8.0 %collective-permute-done.53.refs_2_ = bf16[128,1536]{1,0:T(8,128)(2,1)S(1)} collective-permute-done((bf16[128,1536]{1,0:T(8,128)(2,1)S(1)}, bf16[128,1536]{1,0:T(8,128)(2,1)S(1)}, u32[]{:S(2)}, u32[]{:S(2)}) %collective-permute-start.53) | collective-permute-done | bytes 393248 | tf_op jit(solution)/shard_map/ppermute | solution.py:260
  215.7 4.0 %collective-permute-done.69.refs_5_ = bf16[128,256]{1,0:T(8,128)(2,1)S(1)} collective-permute-done((bf16[128,256]{1,0:T(8,128)(2,1)S(1)}, bf16[128,256]{1,0:T(8,128)(2,1)S(1)}, u32[]{:S(2)}, u32[]{:S(2)}) %collective-permute-start.69) | collective-permute-done | bytes 65568 | tf_op jit(solution)/shard_map/ppermute | solution.py:269
  219.7 3.1 %collective-permute-start.58 = (bf16[128,256]{1,0:T(8,128)(2,1)S(1)}, bf16[128,256]{1,0:T(8,128)(2,1)S(1)}, u32[]{:S(2)}, u32[]{:S(2)}) collective-permute-start(bf16[128,256]{1,0:T(8,128)(2,1)S(1)} %get-tuple-element.122), channel_id=1, source_target_pairs={{0,16},{4,20},{8,24},{12,28},{16,0},{20,4},{24,8},{28,12},{1,17},{... | collective-permute-start | bytes 196616 | tf_op jit(solution)/shard_map/ppermute | solution.py:269
  226.4 3.3 %collective-permute-start.48 = (bf16[128,256]{1,0:T(8,128)(2,1)S(1)}, bf16[128,256]{1,0:T(8,128)(2,1)S(1)}, u32[]{:S(2)}, u32[]{:S(2)}) collective-permute-start(bf16[128,256]{1,0:T(8,128)(2,1)S(1)} %get-tuple-element.110), channel_id=1, source_target_pairs={{0,16},{4,20},{8,24},{12,28},{16,0},{20,4},{24,8},{28,12},{1,17},{... | collective-permute-start | bytes 196616 | tf_op jit(solution)/shard_map/ppermute | solution.py:269
  229.7 3.0 %collective-permute-done.59.refs_5_ = bf16[128,256]{1,0:T(8,128)(2,1)S(1)} collective-permute-done((bf16[128,256]{1,0:T(8,128)(2,1)S(1)}, bf16[128,256]{1,0:T(8,128)(2,1)S(1)}, u32[]{:S(2)}, u32[]{:S(2)}) %collective-permute-start.59) | collective-permute-done | bytes 65568 | tf_op jit(solution)/shard_map/ppermute | solution.py:269
  239.2 2.4 collective-permute-done.48.refs_4_
  241.6 2.4 collective-permute-done.49.refs_5_
  (190 shorter events, 117.6 us)
Async XLA Ops:
  25.2 19.6 %collective-permute-start.9 = (bf16[256,256]{1,0:T(8,128)(2,1)S(1)}, bf16[256,256]{1,0:T(8,128)(2,1)S(1)}, u32[]{:S(2)}, u32[]{:S(2)}) collective-permute-start(bf16[256,256]{1,0:T(8,128)(2,1)S(1)} %get-tuple-element.170), channel_id=1, source_target_pairs={{0,28},{4,24},{8,20},{12,16},{16,12},{20,8},{24,4},{28,0},{1,29},{... | collective-permute-start | bytes 393224 | tf_op jit(solution)/shard_map/ppermute | solution.py:269
  27.3 16.1 %collective-permute-start.21 = (bf16[128,256]{1,0:T(8,128)(2,1)S(1)}, bf16[128,256]{1,0:T(8,128)(2,1)S(1)}, u32[]{:S(2)}, u32[]{:S(2)}) collective-permute-start(bf16[128,256]{1,0:T(8,128)(2,1)S(1)} %get-tuple-element.165), channel_id=1, source_target_pairs={{0,12},{4,8},{8,4},{12,0},{16,28},{20,24},{24,20},{28,16},{1,13},{... | collective-permute-start | bytes 196616 | tf_op jit(solution)/shard_map/ppermute | solution.py:269
  27.3 16.5 %collective-permute-start.20 = (bf16[128,256]{1,0:T(8,128)(2,1)S(1)}, bf16[128,256]{1,0:T(8,128)(2,1)S(1)}, u32[]{:S(2)}, u32[]{:S(2)}) collective-permute-start(bf16[128,256]{1,0:T(8,128)(2,1)S(1)} %get-tuple-element.166), channel_id=1, source_target_pairs={{0,8},{4,12},{8,0},{12,4},{16,24},{20,28},{24,16},{28,20},{1,9},{5... | collective-permute-start | bytes 196616 | tf_op jit(solution)/shard_map/ppermute | solution.py:269
  43.4 19.8 %collective-permute-start.36 = (bf16[128,1536]{1,0:T(8,128)(2,1)S(1)}, bf16[128,1536]{1,0:T(8,128)(2,1)S(1)}, u32[]{:S(2)}, u32[]{:S(2)}) collective-permute-start(bf16[128,1536]{1,0:T(8,128)(2,1)S(1)} %get-tuple-element.95), channel_id=1, source_target_pairs={{0,1},{1,0},{2,3},{3,2},{4,5},{5,4},{6,7},{7,6},{8,9},{9,8},{10,11... | collective-permute-start | bytes 1179656 | tf_op jit(solution)/shard_map/ppermute | solution.py:260
  43.8 14.5 %collective-permute-start.6 = (bf16[256,256]{1,0:T(8,128)(2,1)S(1)}, bf16[256,256]{1,0:T(8,128)(2,1)S(1)}, u32[]{:S(2)}, u32[]{:S(2)}) collective-permute-start(bf16[256,256]{1,0:T(8,128)(2,1)S(1)} %get-tuple-element.173), channel_id=1, source_target_pairs={{0,16},{4,20},{8,24},{12,28},{16,0},{20,4},{24,8},{28,12},{1,17},{... | collective-permute-start | bytes 393224 | tf_op jit(solution)/shard_map/ppermute | solution.py:269
  44.7 14.3 %collective-permute-start.5 = (bf16[256,256]{1,0:T(8,128)(2,1)S(1)}, bf16[256,256]{1,0:T(8,128)(2,1)S(1)}, u32[]{:S(2)}, u32[]{:S(2)}) collective-permute-start(bf16[256,256]{1,0:T(8,128)(2,1)S(1)} %get-tuple-element.174), channel_id=1, source_target_pairs={{0,12},{4,8},{8,4},{12,0},{16,28},{20,24},{24,20},{28,16},{1,13},{... | collective-permute-start | bytes 393224 | tf_op jit(solution)/shard_map/ppermute | solution.py:269
  55.2 20.4 %collective-permute-start.37 = (bf16[128,1536]{1,0:T(8,128)(2,1)S(1)}, bf16[128,1536]{1,0:T(8,128)(2,1)S(1)}, u32[]{:S(2)}, u32[]{:S(2)}) collective-permute-start(bf16[128,1536]{1,0:T(8,128)(2,1)S(1)} %get-tuple-element.96), channel_id=1, source_target_pairs={{0,2},{1,3},{2,0},{3,1},{4,6},{5,7},{6,4},{7,5},{8,10},{9,11},{10,... | collective-permute-start | bytes 1179656 | tf_op jit(solution)/shard_map/ppermute | solution.py:260
  58.3 18.4 %collective-permute-start.38 = (bf16[128,1536]{1,0:T(8,128)(2,1)S(1)}, bf16[128,1536]{1,0:T(8,128)(2,1)S(1)}, u32[]{:S(2)}, u32[]{:S(2)}) collective-permute-start(bf16[128,1536]{1,0:T(8,128)(2,1)S(1)} %get-tuple-element.97), channel_id=1, source_target_pairs={{0,3},{1,2},{2,1},{3,0},{4,7},{5,6},{6,5},{7,4},{8,11},{9,10},{10,... | collective-permute-start | bytes 1179656 | tf_op jit(solution)/shard_map/ppermute | solution.py:260
  59.0 20.7 %collective-permute-start.26 = (bf16[128,1536]{1,0:T(8,128)(2,1)S(1)}, bf16[128,1536]{1,0:T(8,128)(2,1)S(1)}, u32[]{:S(2)}, u32[]{:S(2)}) collective-permute-start(bf16[128,1536]{1,0:T(8,128)(2,1)S(1)} %get-tuple-element.91), channel_id=1, source_target_pairs={{0,1},{1,0},{2,3},{3,2},{4,5},{5,4},{6,7},{7,6},{8,9},{9,8},{10,11... | collective-permute-start | bytes 1179656 | tf_op jit(solution)/shard_map/ppermute | solution.py:260
  62.7 29.8 %collective-permute-start.27 = (bf16[128,1536]{1,0:T(8,128)(2,1)S(1)}, bf16[128,1536]{1,0:T(8,128)(2,1)S(1)}, u32[]{:S(2)}, u32[]{:S(2)}) collective-permute-start(bf16[128,1536]{1,0:T(8,128)(2,1)S(1)} %get-tuple-element.92), channel_id=1, source_target_pairs={{0,2},{1,3},{2,0},{3,1},{4,6},{5,7},{6,4},{7,5},{8,10},{9,11},{10,... | collective-permute-start | bytes 1179656 | tf_op jit(solution)/shard_map/ppermute | solution.py:260
  63.2 30.4 %collective-permute-start.28 = (bf16[128,1536]{1,0:T(8,128)(2,1)S(1)}, bf16[128,1536]{1,0:T(8,128)(2,1)S(1)}, u32[]{:S(2)}, u32[]{:S(2)}) collective-permute-start(bf16[128,1536]{1,0:T(8,128)(2,1)S(1)} %get-tuple-element.93), channel_id=1, source_target_pairs={{0,3},{1,2},{2,1},{3,0},{4,7},{5,6},{6,5},{7,4},{8,11},{9,10},{10,... | collective-permute-start | bytes 1179656 | tf_op jit(solution)/shard_map/ppermute | solution.py:260
  75.7 32.8 %collective-permute-start.16 = (bf16[128,1536]{1,0:T(8,128)(2,1)S(1)}, bf16[128,1536]{1,0:T(8,128)(2,1)S(1)}, u32[]{:S(2)}, u32[]{:S(2)}) collective-permute-start(bf16[128,1536]{1,0:T(8,128)(2,1)S(1)} %get-tuple-element.87), channel_id=1, source_target_pairs={{0,1},{1,0},{2,3},{3,2},{4,5},{5,4},{6,7},{7,6},{8,9},{9,8},{10,11... | collective-permute-start | bytes 1179656 | tf_op jit(solution)/shard_map/ppermute | solution.py:260
  76.7 33.5 %collective-permute-start.17 = (bf16[128,1536]{1,0:T(8,128)(2,1)S(1)}, bf16[128,1536]{1,0:T(8,128)(2,1)S(1)}, u32[]{:S(2)}, u32[]{:S(2)}) collective-permute-start(bf16[128,1536]{1,0:T(8,128)(2,1)S(1)} %get-tuple-element.88), channel_id=1, source_target_pairs={{0,2},{1,3},{2,0},{3,1},{4,6},{5,7},{6,4},{7,5},{8,10},{9,11},{10,... | collective-permute-start | bytes 1179656 | tf_op jit(solution)/shard_map/ppermute | solution.py:260
  79.7 32.0 %collective-permute-start.18 = (bf16[128,1536]{1,0:T(8,128)(2,1)S(1)}, bf16[128,1536]{1,0:T(8,128)(2,1)S(1)}, u32[]{:S(2)}, u32[]{:S(2)}) collective-permute-start(bf16[128,1536]{1,0:T(8,128)(2,1)S(1)} %get-tuple-element.89), channel_id=1, source_target_pairs={{0,3},{1,2},{2,1},{3,0},{4,7},{5,6},{6,5},{7,4},{8,11},{9,10},{10,... | collective-permute-start | bytes 1179656 | tf_op jit(solution)/shard_map/ppermute | solution.py:260
  92.5 15.7 %collective-permute-start.13 = (bf16[64,1536]{1,0:T(8,128)(2,1)S(1)}, bf16[64,1536]{1,0:T(8,128)(2,1)S(1)}, u32[]{:S(2)}, u32[]{:S(2)}) collective-permute-start(bf16[64,1536]{1,0:T(8,128)(2,1)S(1)} %get-tuple-element.83), channel_id=1, source_target_pairs={{0,1},{1,0},{2,3},{3,2},{4,5},{5,4},{6,7},{7,6},{8,9},{9,8},{10,11... | collective-permute-start | bytes 589832 | tf_op jit(solution)/shard_map/ppermute | solution.py:260
  93.6 24.7 %collective-permute-start.14 = (bf16[64,1536]{1,0:T(8,128)(2,1)S(1)}, bf16[64,1536]{1,0:T(8,128)(2,1)S(1)}, u32[]{:S(2)}, u32[]{:S(2)}) collective-permute-start(bf16[64,1536]{1,0:T(8,128)(2,1)S(1)} %get-tuple-element.84), channel_id=1, source_target_pairs={{0,2},{1,3},{2,0},{3,1},{4,6},{5,7},{6,4},{7,5},{8,10},{9,11},{10,... | collective-permute-start | bytes 589832 | tf_op jit(solution)/shard_map/ppermute | solution.py:260
  110.2 15.4 %collective-permute-start.11 = (bf16[64,1536]{1,0:T(8,128)(2,1)S(1)}, bf16[64,1536]{1,0:T(8,128)(2,1)S(1)}, u32[]{:S(2)}, u32[]{:S(2)}) collective-permute-start(bf16[64,1536]{1,0:T(8,128)(2,1)S(1)} %get-tuple-element.80), channel_id=1, source_target_pairs={{0,2},{1,3},{2,0},{3,1},{4,6},{5,7},{6,4},{7,5},{8,10},{9,11},{10,... | collective-permute-start | bytes 589832 | tf_op jit(solution)/shard_map/ppermute | solution.py:260
  111.7 13.8 %collective-permute-start.12 = (bf16[64,1536]{1,0:T(8,128)(2,1)S(1)}, bf16[64,1536]{1,0:T(8,128)(2,1)S(1)}, u32[]{:S(2)}, u32[]{:S(2)}) collective-permute-start(bf16[64,1536]{1,0:T(8,128)(2,1)S(1)} %get-tuple-element.81), channel_id=1, source_target_pairs={{0,3},{1,2},{2,1},{3,0},{4,7},{5,6},{6,5},{7,4},{8,11},{9,10},{10,... | collective-permute-start | bytes 589832 | tf_op jit(solution)/shard_map/ppermute | solution.py:260
  134.5 14.7 %collective-permute-start.77 = (bf16[64,1536]{1,0:T(8,128)(2,1)S(1)}, bf16[64,1536]{1,0:T(8,128)(2,1)S(1)}, u32[]{:S(2)}, u32[]{:S(2)}) collective-permute-start(bf16[64,1536]{1,0:T(8,128)(2,1)S(1)} %get-tuple-element.145), channel_id=1, source_target_pairs={{0,3},{1,2},{2,1},{3,0},{4,7},{5,6},{6,5},{7,4},{8,11},{9,10},{10,... | collective-permute-start | bytes 589832 | tf_op jit(solution)/shard_map/ppermute | solution.py:260
  149.3 14.2 %collective-permute-start.43 = (bf16[64,1536]{1,0:T(8,128)(2,1)S(1)}, bf16[64,1536]{1,0:T(8,128)(2,1)S(1)}, u32[]{:S(2)}, u32[]{:S(2)}) collective-permute-start(bf16[64,1536]{1,0:T(8,128)(2,1)S(1)} %get-tuple-element.104), channel_id=1, source_target_pairs={{0,2},{1,3},{2,0},{3,1},{4,6},{5,7},{6,4},{7,5},{8,10},{9,11},{10,... | collective-permute-start | bytes 589832 | tf_op jit(solution)/shard_map/ppermute | solution.py:260
  150.8 15.8 %collective-permute-start.44 = (bf16[64,1536]{1,0:T(8,128)(2,1)S(1)}, bf16[64,1536]{1,0:T(8,128)(2,1)S(1)}, u32[]{:S(2)}, u32[]{:S(2)}) collective-permute-start(bf16[64,1536]{1,0:T(8,128)(2,1)S(1)} %get-tuple-element.105), channel_id=1, source_target_pairs={{0,3},{1,2},{2,1},{3,0},{4,7},{5,6},{6,5},{7,4},{8,11},{9,10},{10,... | collective-permute-start | bytes 589832 | tf_op jit(solution)/shard_map/ppermute | solution.py:260
  155.3 13.7 %collective-permute-start.40 = (bf16[64,1536]{1,0:T(8,128)(2,1)S(1)}, bf16[64,1536]{1,0:T(8,128)(2,1)S(1)}, u32[]{:S(2)}, u32[]{:S(2)}) collective-permute-start(bf16[64,1536]{1,0:T(8,128)(2,1)S(1)} %get-tuple-element.100), channel_id=1, source_target_pairs={{0,2},{1,3},{2,0},{3,1},{4,6},{5,7},{6,4},{7,5},{8,10},{9,11},{10,... | collective-permute-start | bytes 589832 | tf_op jit(solution)/shard_map/ppermute | solution.py:260
  157.7 13.6 %collective-permute-start.41 = (bf16[64,1536]{1,0:T(8,128)(2,1)S(1)}, bf16[64,1536]{1,0:T(8,128)(2,1)S(1)}, u32[]{:S(2)}, u32[]{:S(2)}) collective-permute-start(bf16[64,1536]{1,0:T(8,128)(2,1)S(1)} %get-tuple-element.101), channel_id=1, source_target_pairs={{0,3},{1,2},{2,1},{3,0},{4,7},{5,6},{6,5},{7,4},{8,11},{9,10},{10,... | collective-permute-start | bytes 589832 | tf_op jit(solution)/shard_map/ppermute | solution.py:260
  163.5 21.7 %collective-permute-start.62 = (bf16[128,1536]{1,0:T(8,128)(2,1)S(1)}, bf16[128,1536]{1,0:T(8,128)(2,1)S(1)}, u32[]{:S(2)}, u32[]{:S(2)}) collective-permute-start(bf16[128,1536]{1,0:T(8,128)(2,1)S(1)} %get-tuple-element.127), channel_id=1, source_target_pairs={{0,1},{1,0},{2,3},{3,2},{4,5},{5,4},{6,7},{7,6},{8,9},{9,8},{10,11... | collective-permute-start | bytes 1179656 | tf_op jit(solution)/shard_map/ppermute | solution.py:260
  171.3 20.4 %collective-permute-start.63 = (bf16[128,1536]{1,0:T(8,128)(2,1)S(1)}, bf16[128,1536]{1,0:T(8,128)(2,1)S(1)}, u32[]{:S(2)}, u32[]{:S(2)}) collective-permute-start(bf16[128,1536]{1,0:T(8,128)(2,1)S(1)} %get-tuple-element.128), channel_id=1, source_target_pairs={{0,2},{1,3},{2,0},{3,1},{4,6},{5,7},{6,4},{7,5},{8,10},{9,11},{10,... | collective-permute-start | bytes 1179656 | tf_op jit(solution)/shard_map/ppermute | solution.py:260
  171.9 19.9 %collective-permute-start.64 = (bf16[128,1536]{1,0:T(8,128)(2,1)S(1)}, bf16[128,1536]{1,0:T(8,128)(2,1)S(1)}, u32[]{:S(2)}, u32[]{:S(2)}) collective-permute-start(bf16[128,1536]{1,0:T(8,128)(2,1)S(1)} %get-tuple-element.129), channel_id=1, source_target_pairs={{0,3},{1,2},{2,1},{3,0},{4,7},{5,6},{6,5},{7,4},{8,11},{9,10},{10,... | collective-permute-start | bytes 1179656 | tf_op jit(solution)/shard_map/ppermute | solution.py:260
  182.8 16.1 %collective-permute-start.52 = (bf16[128,1536]{1,0:T(8,128)(2,1)S(1)}, bf16[128,1536]{1,0:T(8,128)(2,1)S(1)}, u32[]{:S(2)}, u32[]{:S(2)}) collective-permute-start(bf16[128,1536]{1,0:T(8,128)(2,1)S(1)} %get-tuple-element.115), channel_id=1, source_target_pairs={{0,1},{1,0},{2,3},{3,2},{4,5},{5,4},{6,7},{7,6},{8,9},{9,8},{10,11... | collective-permute-start | bytes 1179656 | tf_op jit(solution)/shard_map/ppermute | solution.py:260
  183.9 23.5 %collective-permute-start.53 = (bf16[128,1536]{1,0:T(8,128)(2,1)S(1)}, bf16[128,1536]{1,0:T(8,128)(2,1)S(1)}, u32[]{:S(2)}, u32[]{:S(2)}) collective-permute-start(bf16[128,1536]{1,0:T(8,128)(2,1)S(1)} %get-tuple-element.116), channel_id=1, source_target_pairs={{0,2},{1,3},{2,0},{3,1},{4,6},{5,7},{6,4},{7,5},{8,10},{9,11},{10,... | collective-permute-start | bytes 1179656 | tf_op jit(solution)/shard_map/ppermute | solution.py:260
  185.2 22.1 %collective-permute-start.54 = (bf16[128,1536]{1,0:T(8,128)(2,1)S(1)}, bf16[128,1536]{1,0:T(8,128)(2,1)S(1)}, u32[]{:S(2)}, u32[]{:S(2)}) collective-permute-start(bf16[128,1536]{1,0:T(8,128)(2,1)S(1)} %get-tuple-element.117), channel_id=1, source_target_pairs={{0,3},{1,2},{2,1},{3,0},{4,7},{5,6},{6,5},{7,4},{8,11},{9,10},{10,... | collective-permute-start | bytes 1179656 | tf_op jit(solution)/shard_map/ppermute | solution.py:260
  197.3 13.3 %collective-permute-start.46 = (bf16[128,256]{1,0:T(8,128)(2,1)S(1)}, bf16[128,256]{1,0:T(8,128)(2,1)S(1)}, u32[]{:S(2)}, u32[]{:S(2)}) collective-permute-start(bf16[128,256]{1,0:T(8,128)(2,1)S(1)} %get-tuple-element.108), channel_id=1, source_target_pairs={{0,8},{4,12},{8,0},{12,4},{16,24},{20,28},{24,16},{28,20},{1,9},{5... | collective-permute-start | bytes 196616 | tf_op jit(solution)/shard_map/ppermute | solution.py:269
  198.9 14.3 %collective-permute-start.66 = (bf16[128,256]{1,0:T(8,128)(2,1)S(1)}, bf16[128,256]{1,0:T(8,128)(2,1)S(1)}, u32[]{:S(2)}, u32[]{:S(2)}) collective-permute-start(bf16[128,256]{1,0:T(8,128)(2,1)S(1)} %get-tuple-element.132), channel_id=1, source_target_pairs={{0,8},{4,12},{8,0},{12,4},{16,24},{20,28},{24,16},{28,20},{1,9},{5... | collective-permute-start | bytes 196616 | tf_op jit(solution)/shard_map/ppermute | solution.py:269
  226.4 15.2 %collective-permute-start.48 = (bf16[128,256]{1,0:T(8,128)(2,1)S(1)}, bf16[128,256]{1,0:T(8,128)(2,1)S(1)}, u32[]{:S(2)}, u32[]{:S(2)}) collective-permute-start(bf16[128,256]{1,0:T(8,128)(2,1)S(1)} %get-tuple-element.110), channel_id=1, source_target_pairs={{0,16},{4,20},{8,24},{12,28},{16,0},{20,4},{24,8},{28,12},{1,17},{... | collective-permute-start | bytes 196616 | tf_op jit(solution)/shard_map/ppermute | solution.py:269
  (63 other events, 633.4 us)
where the time goes:
time: 247 us; the launch traced here: 246 us
  starting transfers between devices  99.3 us (40%)
  waiting for transfers between devices  79.4 us (32%)
  Pallas kernels  59.2 us (24%)
  local copies, waits for them, and re-layouts  5.88 us (2%)
    ppermute x49, starting transfers between devices, across(): lax.ppermute(values[d], 'mat', [(i, i ^ d) for i in range(n_mat)])  53.9 us
    ppermute x36, starting transfers between devices, to_peer(): return lax.ppermute(value, 'pts', [(i, i ^ o) for i in range(n_pts)])  45.4 us
    ppermute x36, waiting for transfers between devices, to_peer(): return lax.ppermute(value, 'pts', [(i, i ^ o) for i in range(n_pts)])  45.1 us
    ppermute x49, waiting for transfers between devices, across(): lax.ppermute(values[d], 'mat', [(i, i ^ d) for i in range(n_mat)])  34.3 us
    pallas_call x6, Pallas kernels, response(): pl.pallas_call(functools.partial(response_kernel, dims, start, rows, 256)...  21.1 us
    pallas_call x5, Pallas kernels, density(): pl.pallas_call(functools.partial(density_kernel, dims, start, rows, 256,...  19.2 us
    pallas_call x4, Pallas kernels, widen(): pl.pallas_call(functools.partial(widen_kernel, n_mat), out_shape=jax.Shap...  6.4 us
    pallas_call x4, Pallas kernels, combine(): pl.pallas_call(functools.partial(combine_kernel, dims, strips), out_shape...  5.84 us
  transfers between devices with their start and end apart: 85, of which 26 were waited for; matrix products, arithmetic and copies ran while one was open for 1% of the time, Pallas kernels for 21%

commit v1 on v0

--- a/solution.py
+++ b/solution.py
@@ -245,7 +245,7 @@
 
 def plan_of(row_blocks):
     inward = chunks(row_blocks, [[2], [2], [2, 1, 1]])
-    outward = chunks(row_blocks, [[1, 1], [2], [2], [1, 1]])
+    outward = chunks(row_blocks, [[2], [2], [2], [2]])
     return inward, outward
 
 
@@ -264,9 +264,9 @@
     own_active = active_blocks[0, 0]
 
     def across(values):
-        out = [values[0]]
-        for d in range(1, n_mat):
-            out.append(lax.ppermute(values[d], "mat", [(i, i ^ d) for i in range(n_mat)]))
+        out = [values[0]] + [None] * (n_mat - 1)
+        for d in range(n_mat - 1, 0, -1):
+            out[d] = lax.ppermute(values[d], "mat", [(i, i ^ d) for i in range(n_mat)])
         return out
 
     arrived = {}

time: 247 us -> 254 us (1.028)
  waiting for transfers between devices: 79.4 us -> 85.1 us
  starting transfers between devices: 99.3 us -> 104 us
  Pallas kernels: 59.2 us -> 55.6 us
    ppermute x36 -> x30, waiting for transfers between devices: 45.1 us -> 57.3 us  [to_peer(): return lax.ppermute(value, 'pts', [(i, i ^ o) for i in range(n_pts)])]
    ppermute x49, starting transfers between devices: 53.9 us -> 62.4 us  [across(): out[d] = lax.ppermute(values[d], 'mat', [(i, i ^ d) for i in range(n_mat)])]
    ppermute x49, waiting for transfers between devices: 34.3 us -> 27.8 us  [across(): out[d] = lax.ppermute(values[d], 'mat', [(i, i ^ d) for i in range(n_mat)])]
    ppermute x36 -> x30, starting transfers between devices: 45.4 us -> 41.4 us  [to_peer(): return lax.ppermute(value, 'pts', [(i, i ^ o) for i in range(n_pts)])]
    pallas_call x6 -> x4, Pallas kernels: 21.1 us -> 17.9 us  [response(): pl.pallas_call(functools.partial(response_kernel, dims, start, rows, 256)...]
  transfers between devices with their start and end apart: 85 -> 79, of which waited for: 26 -> 25; matrix products, arithmetic and copies ran while one was open for 1% -> 1% of each run, Pallas kernels for 21% -> 18%
where the time goes in v1:
time: 254 us; the launch traced here: 252 us
  starting transfers between devices  104 us (41%)
  waiting for transfers between devices  85.1 us (34%)
  Pallas kernels  55.6 us (22%)
  local copies, waits for them, and re-layouts  5.88 us (2%)
    ppermute x49, starting transfers between devices, across(): out[d] = lax.ppermute(values[d], 'mat', [(i, i ^ d) for i in range(n_mat)])  62.4 us
    ppermute x30, waiting for transfers between devices, to_peer(): return lax.ppermute(value, 'pts', [(i, i ^ o) for i in range(n_pts)])  57.3 us
    ppermute x30, starting transfers between devices, to_peer(): return lax.ppermute(value, 'pts', [(i, i ^ o) for i in range(n_pts)])  41.4 us
    ppermute x49, waiting for transfers between devices, across(): out[d] = lax.ppermute(values[d], 'mat', [(i, i ^ d) for i in range(n_mat)])  27.8 us
    pallas_call x5, Pallas kernels, density(): pl.pallas_call(functools.partial(density_kernel, dims, start, rows, 256,...  19.2 us
    pallas_call x4, Pallas kernels, response(): pl.pallas_call(functools.partial(response_kernel, dims, start, rows, 256)...  17.9 us
    pallas_call x4, Pallas kernels, widen(): pl.pallas_call(functools.partial(widen_kernel, n_mat), out_shape=jax.Shap...  6.4 us
    pallas_call x4, Pallas kernels, combine(): pl.pallas_call(functools.partial(combine_kernel, dims, strips), out_shape...  5.48 us
  transfers between devices with their start and end apart: 79, of which 25 were waited for; matrix products, arithmetic and copies ran while one was open for 1% of the time, Pallas kernels for 18%

profile of v1, /device:TPU:0, one launch (start us, length us, event | category | flops | bytes accessed | tf_op | source)
XLA Modules:
  0.0 252.0 jit_solution(2739514900028436535)
XLA Ops:
  0.7 4.0 %collective-permute-start.2 = (s32[12]{0:T(128)}, s32[12]{0:T(128)S(1)}, u32[]{:S(2)}, u32[]{:S(2)}) collective-permute-start(s32[12]{0:T(128)} %bitcast.61), channel_id=1, source_target_pairs={{0,3},{1,2},{2,1},{3,0},{4,7},{5,6},{6,5},{7,4},{8,11},{9,10},{10,... | collective-permute-start | bytes 152 | tf_op jit(solution)/shard_map/ppermute | solution.py:260
  6.5 2.5 %collective-permute-start.35 = (bf16[128,256]{1,0:T(8,128)(2,1)S(1)}, bf16[128,256]{1,0:T(8,128)(2,1)S(1)}, u32[]{:S(2)}, u32[]{:S(2)}) collective-permute-start(bf16[128,256]{1,0:T(8,128)(2,1)S(1)} %get-tuple-element.138), channel_id=1, source_target_pairs={{0,28},{4,24},{8,20},{12,16},{16,12},{20,8},{24,4},{28,0},{1,29},{... | collective-permute-start | bytes 196616 | tf_op jit(solution)/shard_map/ppermute | solution.py:269
  9.5 3.5 %collective-permute-start.32 = (bf16[128,256]{1,0:T(8,128)(2,1)S(1)}, bf16[128,256]{1,0:T(8,128)(2,1)S(1)}, u32[]{:S(2)}, u32[]{:S(2)}) collective-permute-start(bf16[128,256]{1,0:T(8,128)(2,1)S(1)} %get-tuple-element.140), channel_id=1, source_target_pairs={{0,16},{4,20},{8,24},{12,28},{16,0},{20,4},{24,8},{28,12},{1,17},{... | collective-permute-start | bytes 196616 | tf_op jit(solution)/shard_map/ppermute | solution.py:269
  14.9 2.6 %collective-permute-done.33.refs_5_ = bf16[128,256]{1,0:T(8,128)(2,1)S(1)} collective-permute-done((bf16[128,256]{1,0:T(8,128)(2,1)S(1)}, bf16[128,256]{1,0:T(8,128)(2,1)S(1)}, u32[]{:S(2)}, u32[]{:S(2)}) %collective-permute-start.33) | collective-permute-done | bytes 65568 | tf_op jit(solution)/shard_map/ppermute | solution.py:269
  29.5 3.2 %collective-permute-done.23.refs_5_ = bf16[128,256]{1,0:T(8,128)(2,1)S(1)} collective-permute-done((bf16[128,256]{1,0:T(8,128)(2,1)S(1)}, bf16[128,256]{1,0:T(8,128)(2,1)S(1)}, u32[]{:S(2)}, u32[]{:S(2)}) %collective-permute-start.23) | collective-permute-done | bytes 65568 | tf_op jit(solution)/shard_map/ppermute | solution.py:269
  36.9 3.6 %collective-permute-done.34.refs_6_ = bf16[128,256]{1,0:T(8,128)(2,1)S(1)} collective-permute-done((bf16[128,256]{1,0:T(8,128)(2,1)S(1)}, bf16[128,256]{1,0:T(8,128)(2,1)S(1)}, u32[]{:S(2)}, u32[]{:S(2)}) %collective-permute-start.34) | collective-permute-done | bytes 65568 | tf_op jit(solution)/shard_map/ppermute | solution.py:269
  48.3 5.1 %collective-permute-start.4 = (bf16[256,256]{1,0:T(8,128)(2,1)S(1)}, bf16[256,256]{1,0:T(8,128)(2,1)S(1)}, u32[]{:S(2)}, u32[]{:S(2)}) collective-permute-start(bf16[256,256]{1,0:T(8,128)(2,1)S(1)} %get-tuple-element.159), channel_id=1, source_target_pairs={{0,8},{4,12},{8,0},{12,4},{16,24},{20,28},{24,16},{28,20},{1,9},{5... | collective-permute-start | bytes 393224 | tf_op jit(solution)/shard_map/ppermute | solution.py:269
  71.1 4.5 %collective-permute-done.37.refs_2_ = bf16[128,1536]{1,0:T(8,128)(2,1)S(1)} collective-permute-done((bf16[128,1536]{1,0:T(8,128)(2,1)S(1)}, bf16[128,1536]{1,0:T(8,128)(2,1)S(1)}, u32[]{:S(2)}, u32[]{:S(2)}) %collective-permute-start.37) | collective-permute-done | bytes 393248 | tf_op jit(solution)/shard_map/ppermute | solution.py:260
  79.7 4.2 %shard_map.100.refs_5_ = f32[1,1536]{1,0:T(1,128)S(1)} custom-call(s32[307]{0:T(512)S(1)} %concatenate.3.meta, bf16[128,1536]{1,0:T(8,128)(2,1)S(1)} %get-tuple-element.86.refs_0_, bf16[128,1536]{1,0:T(8,128)(2,1)S(1)} %collective-permute-done.36.refs_1_, bf16[128,1536]{1,0:T(8,128)(2,1)S(1)} %collective-permute-done.37.refs_2_, ...), custom_call_target="tpu_custom_call" | custom-call | flops 2415919104 | bytes 4718592 | tf_op jit(solution)/shard_map/pallas_call | solution.py:119
  84.0 8.5 %collective-permute-done.27.refs_2_ = bf16[128,1536]{1,0:T(8,128)(2,1)S(1)} collective-permute-done((bf16[128,1536]{1,0:T(8,128)(2,1)S(1)}, bf16[128,1536]{1,0:T(8,128)(2,1)S(1)}, u32[]{:S(2)}, u32[]{:S(2)}) %collective-permute-start.27) | collective-permute-done | bytes 393248 | tf_op jit(solution)/shard_map/ppermute | solution.py:260
  95.1 4.2 %shard_map.101.refs_5_ = f32[1,1536]{1,0:T(1,128)S(1)} custom-call(s32[307]{0:T(512)S(1)} %concatenate.3.meta, bf16[128,1536]{1,0:T(8,128)(2,1)S(1)} %get-tuple-element.82.refs_0_, bf16[128,1536]{1,0:T(8,128)(2,1)S(1)} %collective-permute-done.26.refs_1_, bf16[128,1536]{1,0:T(8,128)(2,1)S(1)} %collective-permute-done.27.refs_2_, ...), custom_call_target="tpu_custom_call" | custom-call | flops 2415919104 | bytes 4718592 | tf_op jit(solution)/shard_map/pallas_call | solution.py:119
  99.3 8.9 %collective-permute-done.13.refs_1_ = bf16[64,1536]{1,0:T(8,128)(2,1)S(1)} collective-permute-done((bf16[64,1536]{1,0:T(8,128)(2,1)S(1)}, bf16[64,1536]{1,0:T(8,128)(2,1)S(1)}, u32[]{:S(2)}, u32[]{:S(2)}) %collective-permute-start.13) | collective-permute-done | bytes 196640 | tf_op jit(solution)/shard_map/ppermute | solution.py:260
  114.0 4.2 %shard_map.102.refs_5_ = f32[1,1536]{1,0:T(1,128)S(1)} custom-call(s32[307]{0:T(512)S(1)} %concatenate.3.meta, bf16[128,1536]{1,0:T(8,128)(2,1)S(1)} %get-tuple-element.78.refs_0_, bf16[128,1536]{1,0:T(8,128)(2,1)S(1)} %collective-permute-done.16.refs_1_, bf16[128,1536]{1,0:T(8,128)(2,1)S(1)} %collective-permute-done.17.refs_2_, ...), custom_call_target="tpu_custom_call" | custom-call | flops 2415919104 | bytes 4718592 | tf_op jit(solution)/shard_map/pallas_call | solution.py:119
  118.3 3.0 %shard_map.103.refs_5_ = f32[1,1536]{1,0:T(1,128)S(1)} custom-call(s32[307]{0:T(512)S(1)} %concatenate.3.meta, bf16[64,1536]{1,0:T(8,128)(2,1)S(1)} %get-tuple-element.74.refs_0_, bf16[64,1536]{1,0:T(8,128)(2,1)S(1)} %collective-permute-done.13.refs_1_, bf16[64,1536]{1,0:T(8,128)(2,1)S(1)} %collective-permute-done.14.refs_2_, ...), custom_call_target="tpu_custom_call" | custom-call | flops 1207959552 | bytes 4718592 | tf_op jit(solution)/shard_map/pallas_call | solution.py:119
  121.3 4.3 %collective-permute-done.11.refs_2_ = bf16[64,1536]{1,0:T(8,128)(2,1)S(1)} collective-permute-done((bf16[64,1536]{1,0:T(8,128)(2,1)S(1)}, bf16[64,1536]{1,0:T(8,128)(2,1)S(1)}, u32[]{:S(2)}, u32[]{:S(2)}) %collective-permute-start.11) | collective-permute-done | bytes 196640 | tf_op jit(solution)/shard_map/ppermute | solution.py:260
  125.5 3.6 %shard_map.104.refs_2_ = f32[1,1536]{1,0:T(1,128)} custom-call(s32[307]{0:T(512)S(1)} %concatenate.3.meta, bf16[64,1536]{1,0:T(8,128)(2,1)S(1)} %get-tuple-element.70.refs_0_, bf16[64,1536]{1,0:T(8,128)(2,1)S(1)} %collective-permute-done.10.refs_1_, bf16[64,1536]{1,0:T(8,128)(2,1)S(1)} %collective-permute-done.11.refs_2_, ...), custom_call_target="tpu_custom_call" | custom-call | flops 1207959552 | bytes 4718592 | tf_op jit(solution)/shard_map/pallas_call | solution.py:119
  129.8 4.4 %shard_map.111 = (bf16[128,1536]{1,0:T(8,128)(2,1)S(1)}, bf16[128,1536]{1,0:T(8,128)(2,1)S(1)}, bf16[128,1536]{1,0:T(8,128)(2,1)S(1)}, bf16[128,1536]{1,0:T(8,128)(2,1)S(1)}) custom-call(s32[307]{0:T(512)S(1)} %concatenate.3.meta, bf16[1536,1536]{1,0:T(8,128)(2,1)S(1)} %flip.1.refs_4_.refs_0_, bf16[1536,1536]{1,0:T(8,128)(2,1)S(1)} %bitcast.57, ...), custom_call_target="tpu_custom_call" | custom-call | flops 2415919104 | bytes 9437184 | tf_op jit(solution)/shard_map/pallas_call | solution.py:154
  137.8 4.4 %shard_map.109 = (bf16[128,1536]{1,0:T(8,128)(2,1)S(1)}, bf16[128,1536]{1,0:T(8,128)(2,1)S(1)}, bf16[128,1536]{1,0:T(8,128)(2,1)S(1)}, bf16[128,1536]{1,0:T(8,128)(2,1)S(1)}) custom-call(s32[307]{0:T(512)S(1)} %concatenate.3.meta, bf16[1536,1536]{1,0:T(8,128)(2,1)S(1)} %flip.1.refs_4_.refs_0_, bf16[1536,1536]{1,0:T(8,128)(2,1)S(1)} %bitcast.58, ...), custom_call_target="tpu_custom_call" | custom-call | flops 2415919104 | bytes 9437184 | tf_op jit(solution)/shard_map/pallas_call | solution.py:154
  143.9 4.4 %shard_map.107 = (bf16[128,1536]{1,0:T(8,128)(2,1)S(1)}, bf16[128,1536]{1,0:T(8,128)(2,1)S(1)}, bf16[128,1536]{1,0:T(8,128)(2,1)S(1)}, bf16[128,1536]{1,0:T(8,128)(2,1)S(1)}) custom-call(s32[307]{0:T(512)S(1)} %concatenate.3.meta, bf16[1536,1536]{1,0:T(8,128)(2,1)S(1)} %flip.1.refs_4_.refs_0_, bf16[1536,1536]{1,0:T(8,128)(2,1)S(1)} %bitcast.59, ...), custom_call_target="tpu_custom_call" | custom-call | flops 2415919104 | bytes 9437184 | tf_op jit(solution)/shard_map/pallas_call | solution.py:154
  150.3 3.1 %collective-permute-done.70.refs_2_ = bf16[128,1536]{1,0:T(8,128)(2,1)S(1)} collective-permute-done((bf16[128,1536]{1,0:T(8,128)(2,1)S(1)}, bf16[128,1536]{1,0:T(8,128)(2,1)S(1)}, u32[]{:S(2)}, u32[]{:S(2)}) %collective-permute-start.70) | collective-permute-done | bytes 393248 | tf_op jit(solution)/shard_map/ppermute | solution.py:260
  153.4 3.1 %collective-permute-start.49 = (bf16[128,1536]{1,0:T(8,128)(2,1)S(1)}, bf16[128,1536]{1,0:T(8,128)(2,1)S(1)}, u32[]{:S(2)}, u32[]{:S(2)}) collective-permute-start(bf16[128,1536]{1,0:T(8,128)(2,1)S(1)} %get-tuple-element.103), channel_id=1, source_target_pairs={{0,1},{1,0},{2,3},{3,2},{4,5},{5,4},{6,7},{7,6},{8,9},{9,8},{10,11... | collective-permute-start | bytes 1179656 | tf_op jit(solution)/shard_map/ppermute | solution.py:260
  156.5 4.6 %shard_map.105 = (bf16[128,1536]{1,0:T(8,128)(2,1)S(1)}, bf16[128,1536]{1,0:T(8,128)(2,1)S(1)}, bf16[128,1536]{1,0:T(8,128)(2,1)S(1)}, bf16[128,1536]{1,0:T(8,128)(2,1)S(1)}) custom-call(s32[307]{0:T(512)S(1)} %concatenate.3.meta, bf16[1536,1536]{1,0:T(8,128)(2,1)S(1)} %flip.1.refs_4_.refs_0_, bf16[1536,1536]{1,0:T(8,128)(2,1)S(1)} %bitcast.60, ...), custom_call_target="tpu_custom_call" | custom-call | flops 2415919104 | bytes 9437184 | tf_op jit(solution)/shard_map/pallas_call | solution.py:154
  164.2 6.0 %collective-permute-done.60.refs_2_ = bf16[128,1536]{1,0:T(8,128)(2,1)S(1)} collective-permute-done((bf16[128,1536]{1,0:T(8,128)(2,1)S(1)}, bf16[128,1536]{1,0:T(8,128)(2,1)S(1)}, u32[]{:S(2)}, u32[]{:S(2)}) %collective-permute-start.60) | collective-permute-done | bytes 393248 | tf_op jit(solution)/shard_map/ppermute | solution.py:260
  170.2 3.1 %collective-permute-start.39 = (bf16[128,1536]{1,0:T(8,128)(2,1)S(1)}, bf16[128,1536]{1,0:T(8,128)(2,1)S(1)}, u32[]{:S(2)}, u32[]{:S(2)}) collective-permute-start(bf16[128,1536]{1,0:T(8,128)(2,1)S(1)} %get-tuple-element.91), channel_id=1, source_target_pairs={{0,1},{1,0},{2,3},{3,2},{4,5},{5,4},{6,7},{7,6},{8,9},{9,8},{10,11... | collective-permute-start | bytes 1179656 | tf_op jit(solution)/shard_map/ppermute | solution.py:260
  175.1 5.0 %collective-permute-done.49.refs_1_ = bf16[128,1536]{1,0:T(8,128)(2,1)S(1)} collective-permute-done((bf16[128,1536]{1,0:T(8,128)(2,1)S(1)}, bf16[128,1536]{1,0:T(8,128)(2,1)S(1)}, u32[]{:S(2)}, u32[]{:S(2)}) %collective-permute-start.49) | collective-permute-done | bytes 393248 | tf_op jit(solution)/shard_map/ppermute | solution.py:260
  182.4 4.6 %collective-permute-done.50.refs_2_ = bf16[128,1536]{1,0:T(8,128)(2,1)S(1)} collective-permute-done((bf16[128,1536]{1,0:T(8,128)(2,1)S(1)}, bf16[128,1536]{1,0:T(8,128)(2,1)S(1)}, u32[]{:S(2)}, u32[]{:S(2)}) %collective-permute-start.50) | collective-permute-done | bytes 393248 | tf_op jit(solution)/shard_map/ppermute | solution.py:260
  189.5 7.5 %collective-permute-done.39.refs_1_ = bf16[128,1536]{1,0:T(8,128)(2,1)S(1)} collective-permute-done((bf16[128,1536]{1,0:T(8,128)(2,1)S(1)}, bf16[128,1536]{1,0:T(8,128)(2,1)S(1)}, u32[]{:S(2)}, u32[]{:S(2)}) %collective-permute-start.39) | collective-permute-done | bytes 393248 | tf_op jit(solution)/shard_map/ppermute | solution.py:260
  198.4 5.8 %collective-permute-start.75 = (bf16[128,256]{1,0:T(8,128)(2,1)S(1)}, bf16[128,256]{1,0:T(8,128)(2,1)S(1)}, u32[]{:S(2)}, u32[]{:S(2)}) collective-permute-start(bf16[128,256]{1,0:T(8,128)(2,1)S(1)} %get-tuple-element.134), channel_id=1, source_target_pairs={{0,16},{4,20},{8,24},{12,28},{16,0},{20,4},{24,8},{28,12},{1,17},{... | collective-permute-start | bytes 196616 | tf_op jit(solution)/shard_map/ppermute | solution.py:269
  208.8 4.2 %collective-permute-done.76.refs_5_ = bf16[128,256]{1,0:T(8,128)(2,1)S(1)} collective-permute-done((bf16[128,256]{1,0:T(8,128)(2,1)S(1)}, bf16[128,256]{1,0:T(8,128)(2,1)S(1)}, u32[]{:S(2)}, u32[]{:S(2)}) %collective-permute-start.76) | collective-permute-done | bytes 65568 | tf_op jit(solution)/shard_map/ppermute | solution.py:269
  213.0 2.8 %collective-permute-start.65 = (bf16[128,256]{1,0:T(8,128)(2,1)S(1)}, bf16[128,256]{1,0:T(8,128)(2,1)S(1)}, u32[]{:S(2)}, u32[]{:S(2)}) collective-permute-start(bf16[128,256]{1,0:T(8,128)(2,1)S(1)} %get-tuple-element.122), channel_id=1, source_target_pairs={{0,16},{4,20},{8,24},{12,28},{16,0},{20,4},{24,8},{28,12},{1,17},{... | collective-permute-start | bytes 196616 | tf_op jit(solution)/shard_map/ppermute | solution.py:269
  223.9 4.3 %collective-permute-start.55 = (bf16[128,256]{1,0:T(8,128)(2,1)S(1)}, bf16[128,256]{1,0:T(8,128)(2,1)S(1)}, u32[]{:S(2)}, u32[]{:S(2)}) collective-permute-start(bf16[128,256]{1,0:T(8,128)(2,1)S(1)} %get-tuple-element.110), channel_id=1, source_target_pairs={{0,16},{4,20},{8,24},{12,28},{16,0},{20,4},{24,8},{28,12},{1,17},{... | collective-permute-start | bytes 196616 | tf_op jit(solution)/shard_map/ppermute | solution.py:269
  233.7 4.5 %collective-permute-done.56.refs_5_ = bf16[128,256]{1,0:T(8,128)(2,1)S(1)} collective-permute-done((bf16[128,256]{1,0:T(8,128)(2,1)S(1)}, bf16[128,256]{1,0:T(8,128)(2,1)S(1)}, u32[]{:S(2)}, u32[]{:S(2)}) %collective-permute-start.56) | collective-permute-done | bytes 65568 | tf_op jit(solution)/shard_map/ppermute | solution.py:269
  (176 shorter events, 108.5 us)
Async XLA Ops:
  25.2 19.6 %collective-permute-start.9 = (bf16[256,256]{1,0:T(8,128)(2,1)S(1)}, bf16[256,256]{1,0:T(8,128)(2,1)S(1)}, u32[]{:S(2)}, u32[]{:S(2)}) collective-permute-start(bf16[256,256]{1,0:T(8,128)(2,1)S(1)} %get-tuple-element.154), channel_id=1, source_target_pairs={{0,28},{4,24},{8,20},{12,16},{16,12},{20,8},{24,4},{28,0},{1,29},{... | collective-permute-start | bytes 393224 | tf_op jit(solution)/shard_map/ppermute | solution.py:269
  27.3 16.1 %collective-permute-start.21 = (bf16[128,256]{1,0:T(8,128)(2,1)S(1)}, bf16[128,256]{1,0:T(8,128)(2,1)S(1)}, u32[]{:S(2)}, u32[]{:S(2)}) collective-permute-start(bf16[128,256]{1,0:T(8,128)(2,1)S(1)} %get-tuple-element.149), channel_id=1, source_target_pairs={{0,12},{4,8},{8,4},{12,0},{16,28},{20,24},{24,20},{28,16},{1,13},{... | collective-permute-start | bytes 196616 | tf_op jit(solution)/shard_map/ppermute | solution.py:269
  27.3 16.5 %collective-permute-start.20 = (bf16[128,256]{1,0:T(8,128)(2,1)S(1)}, bf16[128,256]{1,0:T(8,128)(2,1)S(1)}, u32[]{:S(2)}, u32[]{:S(2)}) collective-permute-start(bf16[128,256]{1,0:T(8,128)(2,1)S(1)} %get-tuple-element.150), channel_id=1, source_target_pairs={{0,8},{4,12},{8,0},{12,4},{16,24},{20,28},{24,16},{28,20},{1,9},{5... | collective-permute-start | bytes 196616 | tf_op jit(solution)/shard_map/ppermute | solution.py:269
  43.4 19.8 %collective-permute-start.36 = (bf16[128,1536]{1,0:T(8,128)(2,1)S(1)}, bf16[128,1536]{1,0:T(8,128)(2,1)S(1)}, u32[]{:S(2)}, u32[]{:S(2)}) collective-permute-start(bf16[128,1536]{1,0:T(8,128)(2,1)S(1)} %get-tuple-element.87), channel_id=1, source_target_pairs={{0,1},{1,0},{2,3},{3,2},{4,5},{5,4},{6,7},{7,6},{8,9},{9,8},{10,11... | collective-permute-start | bytes 1179656 | tf_op jit(solution)/shard_map/ppermute | solution.py:260
  43.8 14.5 %collective-permute-start.6 = (bf16[256,256]{1,0:T(8,128)(2,1)S(1)}, bf16[256,256]{1,0:T(8,128)(2,1)S(1)}, u32[]{:S(2)}, u32[]{:S(2)}) collective-permute-start(bf16[256,256]{1,0:T(8,128)(2,1)S(1)} %get-tuple-element.157), channel_id=1, source_target_pairs={{0,16},{4,20},{8,24},{12,28},{16,0},{20,4},{24,8},{28,12},{1,17},{... | collective-permute-start | bytes 393224 | tf_op jit(solution)/shard_map/ppermute | solution.py:269
  44.7 14.3 %collective-permute-start.5 = (bf16[256,256]{1,0:T(8,128)(2,1)S(1)}, bf16[256,256]{1,0:T(8,128)(2,1)S(1)}, u32[]{:S(2)}, u32[]{:S(2)}) collective-permute-start(bf16[256,256]{1,0:T(8,128)(2,1)S(1)} %get-tuple-element.158), channel_id=1, source_target_pairs={{0,12},{4,8},{8,4},{12,0},{16,28},{20,24},{24,20},{28,16},{1,13},{... | collective-permute-start | bytes 393224 | tf_op jit(solution)/shard_map/ppermute | solution.py:269
  55.2 20.4 %collective-permute-start.37 = (bf16[128,1536]{1,0:T(8,128)(2,1)S(1)}, bf16[128,1536]{1,0:T(8,128)(2,1)S(1)}, u32[]{:S(2)}, u32[]{:S(2)}) collective-permute-start(bf16[128,1536]{1,0:T(8,128)(2,1)S(1)} %get-tuple-element.88), channel_id=1, source_target_pairs={{0,2},{1,3},{2,0},{3,1},{4,6},{5,7},{6,4},{7,5},{8,10},{9,11},{10,... | collective-permute-start | bytes 1179656 | tf_op jit(solution)/shard_map/ppermute | solution.py:260
  58.3 18.4 %collective-permute-start.38 = (bf16[128,1536]{1,0:T(8,128)(2,1)S(1)}, bf16[128,1536]{1,0:T(8,128)(2,1)S(1)}, u32[]{:S(2)}, u32[]{:S(2)}) collective-permute-start(bf16[128,1536]{1,0:T(8,128)(2,1)S(1)} %get-tuple-element.89), channel_id=1, source_target_pairs={{0,3},{1,2},{2,1},{3,0},{4,7},{5,6},{6,5},{7,4},{8,11},{9,10},{10,... | collective-permute-start | bytes 1179656 | tf_op jit(solution)/shard_map/ppermute | solution.py:260
  59.0 20.7 %collective-permute-start.26 = (bf16[128,1536]{1,0:T(8,128)(2,1)S(1)}, bf16[128,1536]{1,0:T(8,128)(2,1)S(1)}, u32[]{:S(2)}, u32[]{:S(2)}) collective-permute-start(bf16[128,1536]{1,0:T(8,128)(2,1)S(1)} %get-tuple-element.83), channel_id=1, source_target_pairs={{0,1},{1,0},{2,3},{3,2},{4,5},{5,4},{6,7},{7,6},{8,9},{9,8},{10,11... | collective-permute-start | bytes 1179656 | tf_op jit(solution)/shard_map/ppermute | solution.py:260
  62.7 29.8 %collective-permute-start.27 = (bf16[128,1536]{1,0:T(8,128)(2,1)S(1)}, bf16[128,1536]{1,0:T(8,128)(2,1)S(1)}, u32[]{:S(2)}, u32[]{:S(2)}) collective-permute-start(bf16[128,1536]{1,0:T(8,128)(2,1)S(1)} %get-tuple-element.84), channel_id=1, source_target_pairs={{0,2},{1,3},{2,0},{3,1},{4,6},{5,7},{6,4},{7,5},{8,10},{9,11},{10,... | collective-permute-start | bytes 1179656 | tf_op jit(solution)/shard_map/ppermute | solution.py:260
  63.2 30.4 %collective-permute-start.28 = (bf16[128,1536]{1,0:T(8,128)(2,1)S(1)}, bf16[128,1536]{1,0:T(8,128)(2,1)S(1)}, u32[]{:S(2)}, u32[]{:S(2)}) collective-permute-start(bf16[128,1536]{1,0:T(8,128)(2,1)S(1)} %get-tuple-element.85), channel_id=1, source_target_pairs={{0,3},{1,2},{2,1},{3,0},{4,7},{5,6},{6,5},{7,4},{8,11},{9,10},{10,... | collective-permute-start | bytes 1179656 | tf_op jit(solution)/shard_map/ppermute | solution.py:260
  75.7 32.8 %collective-permute-start.16 = (bf16[128,1536]{1,0:T(8,128)(2,1)S(1)}, bf16[128,1536]{1,0:T(8,128)(2,1)S(1)}, u32[]{:S(2)}, u32[]{:S(2)}) collective-permute-start(bf16[128,1536]{1,0:T(8,128)(2,1)S(1)} %get-tuple-element.79), channel_id=1, source_target_pairs={{0,1},{1,0},{2,3},{3,2},{4,5},{5,4},{6,7},{7,6},{8,9},{9,8},{10,11... | collective-permute-start | bytes 1179656 | tf_op jit(solution)/shard_map/ppermute | solution.py:260
  76.7 33.5 %collective-permute-start.17 = (bf16[128,1536]{1,0:T(8,128)(2,1)S(1)}, bf16[128,1536]{1,0:T(8,128)(2,1)S(1)}, u32[]{:S(2)}, u32[]{:S(2)}) collective-permute-start(bf16[128,1536]{1,0:T(8,128)(2,1)S(1)} %get-tuple-element.80), channel_id=1, source_target_pairs={{0,2},{1,3},{2,0},{3,1},{4,6},{5,7},{6,4},{7,5},{8,10},{9,11},{10,... | collective-permute-start | bytes 1179656 | tf_op jit(solution)/shard_map/ppermute | solution.py:260
  79.7 32.0 %collective-permute-start.18 = (bf16[128,1536]{1,0:T(8,128)(2,1)S(1)}, bf16[128,1536]{1,0:T(8,128)(2,1)S(1)}, u32[]{:S(2)}, u32[]{:S(2)}) collective-permute-start(bf16[128,1536]{1,0:T(8,128)(2,1)S(1)} %get-tuple-element.81), channel_id=1, source_target_pairs={{0,3},{1,2},{2,1},{3,0},{4,7},{5,6},{6,5},{7,4},{8,11},{9,10},{10,... | collective-permute-start | bytes 1179656 | tf_op jit(solution)/shard_map/ppermute | solution.py:260
  92.5 15.7 %collective-permute-start.13 = (bf16[64,1536]{1,0:T(8,128)(2,1)S(1)}, bf16[64,1536]{1,0:T(8,128)(2,1)S(1)}, u32[]{:S(2)}, u32[]{:S(2)}) collective-permute-start(bf16[64,1536]{1,0:T(8,128)(2,1)S(1)} %get-tuple-element.75), channel_id=1, source_target_pairs={{0,1},{1,0},{2,3},{3,2},{4,5},{5,4},{6,7},{7,6},{8,9},{9,8},{10,11... | collective-permute-start | bytes 589832 | tf_op jit(solution)/shard_map/ppermute | solution.py:260
  93.6 24.7 %collective-permute-start.14 = (bf16[64,1536]{1,0:T(8,128)(2,1)S(1)}, bf16[64,1536]{1,0:T(8,128)(2,1)S(1)}, u32[]{:S(2)}, u32[]{:S(2)}) collective-permute-start(bf16[64,1536]{1,0:T(8,128)(2,1)S(1)} %get-tuple-element.76), channel_id=1, source_target_pairs={{0,2},{1,3},{2,0},{3,1},{4,6},{5,7},{6,4},{7,5},{8,10},{9,11},{10,... | collective-permute-start | bytes 589832 | tf_op jit(solution)/shard_map/ppermute | solution.py:260
  110.2 15.4 %collective-permute-start.11 = (bf16[64,1536]{1,0:T(8,128)(2,1)S(1)}, bf16[64,1536]{1,0:T(8,128)(2,1)S(1)}, u32[]{:S(2)}, u32[]{:S(2)}) collective-permute-start(bf16[64,1536]{1,0:T(8,128)(2,1)S(1)} %get-tuple-element.72), channel_id=1, source_target_pairs={{0,2},{1,3},{2,0},{3,1},{4,6},{5,7},{6,4},{7,5},{8,10},{9,11},{10,... | collective-permute-start | bytes 589832 | tf_op jit(solution)/shard_map/ppermute | solution.py:260
  111.7 13.8 %collective-permute-start.12 = (bf16[64,1536]{1,0:T(8,128)(2,1)S(1)}, bf16[64,1536]{1,0:T(8,128)(2,1)S(1)}, u32[]{:S(2)}, u32[]{:S(2)}) collective-permute-start(bf16[64,1536]{1,0:T(8,128)(2,1)S(1)} %get-tuple-element.73), channel_id=1, source_target_pairs={{0,3},{1,2},{2,1},{3,0},{4,7},{5,6},{6,5},{7,4},{8,11},{9,10},{10,... | collective-permute-start | bytes 589832 | tf_op jit(solution)/shard_map/ppermute | solution.py:260
  134.3 14.1 %collective-permute-start.69 = (bf16[128,1536]{1,0:T(8,128)(2,1)S(1)}, bf16[128,1536]{1,0:T(8,128)(2,1)S(1)}, u32[]{:S(2)}, u32[]{:S(2)}) collective-permute-start(bf16[128,1536]{1,0:T(8,128)(2,1)S(1)} %get-tuple-element.127), channel_id=1, source_target_pairs={{0,1},{1,0},{2,3},{3,2},{4,5},{5,4},{6,7},{7,6},{8,9},{9,8},{10,11... | collective-permute-start | bytes 1179656 | tf_op jit(solution)/shard_map/ppermute | solution.py:260
  134.4 19.0 %collective-permute-start.70 = (bf16[128,1536]{1,0:T(8,128)(2,1)S(1)}, bf16[128,1536]{1,0:T(8,128)(2,1)S(1)}, u32[]{:S(2)}, u32[]{:S(2)}) collective-permute-start(bf16[128,1536]{1,0:T(8,128)(2,1)S(1)} %get-tuple-element.128), channel_id=1, source_target_pairs={{0,2},{1,3},{2,0},{3,1},{4,6},{5,7},{6,4},{7,5},{8,10},{9,11},{10,... | collective-permute-start | bytes 1179656 | tf_op jit(solution)/shard_map/ppermute | solution.py:260
  135.9 25.2 %collective-permute-start.71 = (bf16[128,1536]{1,0:T(8,128)(2,1)S(1)}, bf16[128,1536]{1,0:T(8,128)(2,1)S(1)}, u32[]{:S(2)}, u32[]{:S(2)}) collective-permute-start(bf16[128,1536]{1,0:T(8,128)(2,1)S(1)} %get-tuple-element.129), channel_id=1, source_target_pairs={{0,3},{1,2},{2,1},{3,0},{4,7},{5,6},{6,5},{7,4},{8,11},{9,10},{10,... | collective-permute-start | bytes 1179656 | tf_op jit(solution)/shard_map/ppermute | solution.py:260
  142.3 21.0 %collective-permute-start.59 = (bf16[128,1536]{1,0:T(8,128)(2,1)S(1)}, bf16[128,1536]{1,0:T(8,128)(2,1)S(1)}, u32[]{:S(2)}, u32[]{:S(2)}) collective-permute-start(bf16[128,1536]{1,0:T(8,128)(2,1)S(1)} %get-tuple-element.115), channel_id=1, source_target_pairs={{0,1},{1,0},{2,3},{3,2},{4,5},{5,4},{6,7},{7,6},{8,9},{9,8},{10,11... | collective-permute-start | bytes 1179656 | tf_op jit(solution)/shard_map/ppermute | solution.py:260
  142.4 27.8 %collective-permute-start.60 = (bf16[128,1536]{1,0:T(8,128)(2,1)S(1)}, bf16[128,1536]{1,0:T(8,128)(2,1)S(1)}, u32[]{:S(2)}, u32[]{:S(2)}) collective-permute-start(bf16[128,1536]{1,0:T(8,128)(2,1)S(1)} %get-tuple-element.116), channel_id=1, source_target_pairs={{0,2},{1,3},{2,0},{3,1},{4,6},{5,7},{6,4},{7,5},{8,10},{9,11},{10,... | collective-permute-start | bytes 1179656 | tf_op jit(solution)/shard_map/ppermute | solution.py:260
  148.4 25.0 %collective-permute-start.61 = (bf16[128,1536]{1,0:T(8,128)(2,1)S(1)}, bf16[128,1536]{1,0:T(8,128)(2,1)S(1)}, u32[]{:S(2)}, u32[]{:S(2)}) collective-permute-start(bf16[128,1536]{1,0:T(8,128)(2,1)S(1)} %get-tuple-element.117), channel_id=1, source_target_pairs={{0,3},{1,2},{2,1},{3,0},{4,7},{5,6},{6,5},{7,4},{8,11},{9,10},{10,... | collective-permute-start | bytes 1179656 | tf_op jit(solution)/shard_map/ppermute | solution.py:260
  153.4 26.7 %collective-permute-start.49 = (bf16[128,1536]{1,0:T(8,128)(2,1)S(1)}, bf16[128,1536]{1,0:T(8,128)(2,1)S(1)}, u32[]{:S(2)}, u32[]{:S(2)}) collective-permute-start(bf16[128,1536]{1,0:T(8,128)(2,1)S(1)} %get-tuple-element.103), channel_id=1, source_target_pairs={{0,1},{1,0},{2,3},{3,2},{4,5},{5,4},{6,7},{7,6},{8,9},{9,8},{10,11... | collective-permute-start | bytes 1179656 | tf_op jit(solution)/shard_map/ppermute | solution.py:260
  161.1 25.9 %collective-permute-start.50 = (bf16[128,1536]{1,0:T(8,128)(2,1)S(1)}, bf16[128,1536]{1,0:T(8,128)(2,1)S(1)}, u32[]{:S(2)}, u32[]{:S(2)}) collective-permute-start(bf16[128,1536]{1,0:T(8,128)(2,1)S(1)} %get-tuple-element.104), channel_id=1, source_target_pairs={{0,2},{1,3},{2,0},{3,1},{4,6},{5,7},{6,4},{7,5},{8,10},{9,11},{10,... | collective-permute-start | bytes 1179656 | tf_op jit(solution)/shard_map/ppermute | solution.py:260
  163.2 26.3 %collective-permute-start.51 = (bf16[128,1536]{1,0:T(8,128)(2,1)S(1)}, bf16[128,1536]{1,0:T(8,128)(2,1)S(1)}, u32[]{:S(2)}, u32[]{:S(2)}) collective-permute-start(bf16[128,1536]{1,0:T(8,128)(2,1)S(1)} %get-tuple-element.105), channel_id=1, source_target_pairs={{0,3},{1,2},{2,1},{3,0},{4,7},{5,6},{6,5},{7,4},{8,11},{9,10},{10,... | collective-permute-start | bytes 1179656 | tf_op jit(solution)/shard_map/ppermute | solution.py:260
  170.2 26.8 %collective-permute-start.39 = (bf16[128,1536]{1,0:T(8,128)(2,1)S(1)}, bf16[128,1536]{1,0:T(8,128)(2,1)S(1)}, u32[]{:S(2)}, u32[]{:S(2)}) collective-permute-start(bf16[128,1536]{1,0:T(8,128)(2,1)S(1)} %get-tuple-element.91), channel_id=1, source_target_pairs={{0,1},{1,0},{2,3},{3,2},{4,5},{5,4},{6,7},{7,6},{8,9},{9,8},{10,11... | collective-permute-start | bytes 1179656 | tf_op jit(solution)/shard_map/ppermute | solution.py:260
  173.4 25.0 %collective-permute-start.40 = (bf16[128,1536]{1,0:T(8,128)(2,1)S(1)}, bf16[128,1536]{1,0:T(8,128)(2,1)S(1)}, u32[]{:S(2)}, u32[]{:S(2)}) collective-permute-start(bf16[128,1536]{1,0:T(8,128)(2,1)S(1)} %get-tuple-element.92), channel_id=1, source_target_pairs={{0,2},{1,3},{2,0},{3,1},{4,6},{5,7},{6,4},{7,5},{8,10},{9,11},{10,... | collective-permute-start | bytes 1179656 | tf_op jit(solution)/shard_map/ppermute | solution.py:260
  180.1 24.7 %collective-permute-start.41 = (bf16[128,1536]{1,0:T(8,128)(2,1)S(1)}, bf16[128,1536]{1,0:T(8,128)(2,1)S(1)}, u32[]{:S(2)}, u32[]{:S(2)}) collective-permute-start(bf16[128,1536]{1,0:T(8,128)(2,1)S(1)} %get-tuple-element.93), channel_id=1, source_target_pairs={{0,3},{1,2},{2,1},{3,0},{4,7},{5,6},{6,5},{7,4},{8,11},{9,10},{10,... | collective-permute-start | bytes 1179656 | tf_op jit(solution)/shard_map/ppermute | solution.py:260
  187.0 17.9 %collective-permute-start.72 = (bf16[128,256]{1,0:T(8,128)(2,1)S(1)}, bf16[128,256]{1,0:T(8,128)(2,1)S(1)}, u32[]{:S(2)}, u32[]{:S(2)}) collective-permute-start(bf16[128,256]{1,0:T(8,128)(2,1)S(1)} %get-tuple-element.131), channel_id=1, source_target_pairs={{0,4},{4,0},{8,12},{12,8},{16,20},{20,16},{24,28},{28,24},{1,5},{5... | collective-permute-start | bytes 196616 | tf_op jit(solution)/shard_map/ppermute | solution.py:269
  189.5 17.0 %collective-permute-start.73 = (bf16[128,256]{1,0:T(8,128)(2,1)S(1)}, bf16[128,256]{1,0:T(8,128)(2,1)S(1)}, u32[]{:S(2)}, u32[]{:S(2)}) collective-permute-start(bf16[128,256]{1,0:T(8,128)(2,1)S(1)} %get-tuple-element.132), channel_id=1, source_target_pairs={{0,8},{4,12},{8,0},{12,4},{16,24},{20,28},{24,16},{28,20},{1,9},{5... | collective-permute-start | bytes 196616 | tf_op jit(solution)/shard_map/ppermute | solution.py:269
  (57 other events, 582.7 us)
